TPU v7x, 32 devices: a whole 2x2x4 slice. The times are simulated.
32 devices in a mesh: dom: 8 (over z, core), group: 4 (over y, x).
Axes of the slice: x: 2, y: 2, z: 4, core: 2. Of those that a mesh axis runs over, the one named last changes fastest.
Arguments:
- start: bfloat16 [64, 32768], P(None, ('dom', 'group')), may hold values from -8.1 to 8.1
- tiles: int32 [32, 32, 128, 128], P(('dom', 'group')), may hold values from 0 to 15
- row_ptr: int32 [32, 9], P(('dom', 'group')), may hold values from 0 to 32, as said below
- col_part: int32 [32, 32], P(('dom', 'group')), may hold values from 0 to 7
- col_local: int32 [32, 32], P(('dom', 'group')), may hold values from 0 to 31, as said below
- halo_list: int32 [8, 8, 4], P('dom'), may hold values from 0 to 31
Outputs:
- vectors: bfloat16 [64, 32768], P(None, ('dom', 'group'))
- ritz: float32 [64, 64], replicated
Inputs may be any that keep to these rules, and one draw needn't show every extreme that they name: `row_ptr`: each row is strictly increasing from 0, so every block row has one or more slots; its last entry is at most 32 and equals 32 on some device row. `col_local`: below 32 where col_part names the row's own partition, below 4 otherwise.
All inputs are finite; a program needn't handle non-finite values.
Results may differ from a plain program's by a relative error of at most 0.012.
Values may be sent and summed in bfloat16 or wider, within the bound.
A program may use at most 64 MiB of HBM per device.

v0:
```python
import jax
import jax.numpy as jnp
from jax import lax
from jax.sharding import PartitionSpec as P

ITERS = 2


def shards(start, tiles, row_ptr, col_part, col_local, halo_list):
    own = lax.axis_index("dom")
    n_dom = lax.axis_size("dom")
    n_group = lax.axis_size("group")
    width = start.shape[0]
    rows_dev = start.shape[1]
    block = tiles.shape[2]
    slots = tiles.shape[1]
    block_rows = rows_dev // block
    halo = halo_list.shape[2]
    in_part = block_rows * n_group
    total_rows = rows_dev * n_dom * n_group
    pointers = row_ptr[0]
    counts = (pointers[1:] - pointers[:-1]).astype(jnp.float32)
    row_scale = 1.0 / (4.0 * jnp.sqrt(block * counts))
    slot_ids = jnp.arange(slots, dtype=jnp.int32)
    member = (
        (slot_ids[None, :] >= pointers[:-1, None]) & (slot_ids[None, :] < pointers[1:, None])
    ).astype(jnp.float32)
    centred = (tiles[0].astype(jnp.float32) - 7.5).astype(jnp.bfloat16)
    parts = col_part[0]
    places = col_local[0]
    pool_index = jnp.where(parts == own, places, in_part + parts * halo + places)
    targets = halo_list[0]

    def apply_graph(current):
        shaped = current.reshape(width, block_rows, block)
        part_blocks = lax.all_gather(shaped, "group", axis=1, tiled=True)
        outgoing = jnp.take(part_blocks, targets.reshape(-1), axis=1).reshape(
            width, n_dom, halo, block
        )
        incoming = lax.all_to_all(outgoing, "dom", split_axis=1, concat_axis=1, tiled=True)
        pool = jnp.concatenate([part_blocks, incoming.reshape(width, n_dom * halo, block)], axis=1)
        picked = jnp.take(pool, pool_index, axis=1)
        products = jnp.einsum("ksj,sij->ksi", picked, centred, preferred_element_type=jnp.float32)
        summed = jnp.einsum("rs,ksi->kri", member, products, precision=lax.Precision.HIGHEST)
        return (summed * row_scale[None, :, None]).reshape(width, rows_dev)

    current = start
    for step in range(ITERS):
        image = apply_graph(current)
        rounded = image.astype(jnp.bfloat16)
        local_gram = jnp.einsum("kn,ln->kl", rounded, rounded, preferred_element_type=jnp.float32)
        gram = lax.psum(local_gram, ("dom", "group")) / total_rows
        lower = jnp.linalg.cholesky(gram)
        current = lax.linalg.triangular_solve(
            lower, rounded.astype(jnp.float32), left_side=True, lower=True
        ).astype(jnp.bfloat16)
    final = apply_graph(current)
    local_ritz = jnp.einsum(
        "kn,ln->kl", current.astype(jnp.float32), final, precision=lax.Precision.HIGHEST
    )
    ritz = lax.psum(local_ritz, ("dom", "group")) / total_rows
    return (current, ritz)


def solution(mesh):
    return jax.shard_map(
        shards,
        mesh=mesh,
        in_specs=(
            P(None, ("dom", "group")),
            P(("dom", "group"), None, None, None),
            P(("dom", "group"), None),
            P(("dom", "group"), None),
            P(("dom", "group"), None),
            P("dom", None, None),
        ),
        out_specs=(P(None, ("dom", "group")), P()),
        check_vma=False,
    )
```

profile of v0, /device:TPU:14, one launch (start us, length us, event | category | flops | bytes accessed | tf_op | source)
XLA Modules:
  0.0 251.3 jit_solution(2166994840800570479)
XLA Ops:
  1.7 9.1 %all_gather.9 = bf16[64,32,128]{2,0,1:T(8,128)(2,1)S(1)} all-gather(bf16[64,8,128]{2,0,1:T(8,128)(2,1)S(1)} %copy_bitcast_fusion.2), channel_id=1, replica_groups=mesh['dom'=8,'group'=4] {'group'}, dimensions={1}, use_global_device_ids=true | all-gather | bytes 655360 | tf_op jit(solution)/shard_map/all_gather | solution.py:36
  11.4 0.9 broadcast_select_fusion.2
  12.3 5.5 %all-to-all-start = ((bf16[64,8,4,128]{3,0,2,1:T(8,128)(2,1)}), bf16[64,8,4,128]{3,0,2,1:T(8,128)(2,1)S(1)}, u32[]{:S(2)}, u32[]{:S(2)}) async-start(bf16[64,8,4,128]{3,0,2,1:T(8,128)(2,1)} %bitcast.5), calls=%async_computation | async-start | bytes 1048576 | tf_op jit(solution)/shard_map/all_to_all | solution.py:40
  17.9 11.9 %all-to-all-done = bf16[64,8,4,128]{3,0,2,1:T(8,128)(2,1)S(1)} async-done(((bf16[64,8,4,128]{3,0,2,1:T(8,128)(2,1)}), bf16[64,8,4,128]{3,0,2,1:T(8,128)(2,1)S(1)}, u32[]{:S(2)}, u32[]{:S(2)}) %all-to-all-start) | async-done | bytes 524320 | tf_op jit(solution)/shard_map/all_to_all | solution.py:40
  29.9 1.1 pad_maximum_fusion
  30.9 1.9 gather_fusion.1
  33.7 1.1 fusion.3
  34.9 42.8 %psum.21 = f32[64,64]{0,1:T(8,128)S(1)} all-reduce(f32[64,64]{0,1:T(8,128)S(1)} %convolution_bitcast_fusion.4), channel_id=1, replica_groups=mesh['dom'=8,'group'=4] {'dom','group'}, use_global_device_ids=true, to_apply=%region_0.3 | all-reduce | flops 4096 | bytes 32768 | tf_op jit(solution)/shard_map/psum | solution.py:52
  77.8 5.8 %cholesky.44 = f32[64,64]{1,0:T(8,128)S(1)} custom-call(f32[64,64]{1,0:T(8,128)S(1)} %fusion.35), custom_call_target="Cholesky" | custom-call | tf_op jit(solution)/shard_map/jit(cholesky)/cholesky | solution.py:53
  85.0 4.9 %custom-call.6 = f32[1,64,64]{1,2,0:T(8,128)S(1)} custom-call(f32[1,64,64]{2,1,0:T(8,128)S(1)} %fusion.30), custom_call_target="InvertDiagBlocksLowerTriangular" | custom-call | tf_op jit(solution)/shard_map/triangular_solve/custom-call.0 | solution.py:54
  90.4 9.7 %all_gather.10 = bf16[64,32,128]{2,0,1:T(8,128)(2,1)S(1)} all-gather(bf16[64,8,128]{2,0,1:T(8,128)(2,1)S(1)} %bitcast.125), channel_id=1, replica_groups=mesh['dom'=8,'group'=4] {'group'}, dimensions={1}, use_global_device_ids=true | all-gather | bytes 655360 | tf_op jit(solution)/shard_map/all_gather | solution.py:36
  100.9 16.2 %all_to_all.15 = bf16[64,8,4,128]{3,0,2,1:T(8,128)(2,1)S(1)} all-to-all(bf16[64,8,4,128]{3,0,2,1:T(8,128)(2,1)S(1)} %bitcast.118), channel_id=1, replica_groups=mesh['dom'=8,'group'=4] {'dom'}, dimensions={1} | all-to-all | bytes 1048576 | tf_op jit(solution)/shard_map/all_to_all | solution.py:40
  117.1 1.1 pad_maximum_fusion.1
  118.2 1.9 gather_fusion.3
  120.9 1.1 fusion.2
  122.2 41.9 %psum.22 = f32[64,64]{0,1:T(8,128)S(1)} all-reduce(f32[64,64]{0,1:T(8,128)S(1)} %convolution_bitcast_fusion.3), channel_id=1, replica_groups=mesh['dom'=8,'group'=4] {'dom','group'}, use_global_device_ids=true, to_apply=%region_3.0 | all-reduce | flops 4096 | bytes 32768 | tf_op jit(solution)/shard_map/psum | solution.py:52
  164.2 5.8 %cholesky.55 = f32[64,64]{1,0:T(8,128)S(1)} custom-call(f32[64,64]{1,0:T(8,128)S(1)} %fusion.33), custom_call_target="Cholesky" | custom-call | tf_op jit(solution)/shard_map/jit(cholesky)/cholesky | solution.py:53
  171.4 4.9 %custom-call.7 = f32[1,64,64]{1,2,0:T(8,128)S(1)} custom-call(f32[1,64,64]{2,1,0:T(8,128)S(1)} %fusion.31), custom_call_target="InvertDiagBlocksLowerTriangular" | custom-call | tf_op jit(solution)/shard_map/triangular_solve/custom-call.0 | solution.py:54
  176.8 9.7 %all_gather.11 = bf16[64,32,128]{2,0,1:T(8,128)(2,1)S(1)} all-gather(bf16[64,8,128]{2,0,1:T(8,128)(2,1)S(1)} %copy_bitcast_fusion), channel_id=1, replica_groups=mesh['dom'=8,'group'=4] {'group'}, dimensions={1}, use_global_device_ids=true | all-gather | bytes 655360 | tf_op jit(solution)/shard_map/all_gather | solution.py:36
  187.3 16.2 %all_to_all.16 = bf16[64,8,4,128]{3,0,2,1:T(8,128)(2,1)S(1)} all-to-all(bf16[64,8,4,128]{3,0,2,1:T(8,128)(2,1)S(1)} %bitcast.117), channel_id=1, replica_groups=mesh['dom'=8,'group'=4] {'dom'}, dimensions={1} | all-to-all | bytes 1048576 | tf_op jit(solution)/shard_map/all_to_all | solution.py:40
  203.5 1.1 pad_maximum_fusion.2
  204.6 1.9 gather_fusion.5
  207.3 1.1 convolution_multiply_fusion
  208.7 41.9 %psum.23 = f32[64,64]{0,1:T(8,128)S(1)} all-reduce(f32[64,64]{0,1:T(8,128)S(1)} %fusion.18), channel_id=1, replica_groups=mesh['dom'=8,'group'=4] {'dom','group'}, use_global_device_ids=true, to_apply=%region_4.0 | all-reduce | flops 4096 | bytes 32768 | tf_op jit(solution)/shard_map/psum | solution.py:61
  (53 shorter events, 11.0 us)
Async XLA Ops:
  0.6 1.0 copy-start
  0.6 17.1 %copy-start.5 = (s32[1,32]{1,0:T(1,128)S(1)}, s32[1,32]{1,0:T(1,128)}, u32[]{:S(2)}) copy-start(s32[1,32]{1,0:T(1,128)} %param.17) | copy-start | bytes 388
  0.7 17.1 %copy-start.4 = (s32[1,32]{1,0:T(1,128)S(1)}, s32[1,32]{1,0:T(1,128)}, u32[]{:S(2)}) copy-start(s32[1,32]{1,0:T(1,128)} %param.16) | copy-start | bytes 388
  0.7 17.1 %copy-start.3 = (s32[1,9]{1,0:T(1,128)S(1)}, s32[1,9]{1,0:T(1,128)}, u32[]{:S(2)}) copy-start(s32[1,9]{1,0:T(1,128)} %param.15) | copy-start | bytes 112
  12.3 20.5 %copy-start.1 = (s32[1,32,128,128]{3,2,1,0:T(8,128)S(1)}, s32[1,32,128,128]{3,2,1,0:T(8,128)}, u32[]{:S(2)}) copy-start(s32[1,32,128,128]{3,2,1,0:T(8,128)} %param.14) | copy-start | bytes 6291460
  12.3 17.6 %all-to-all-start = ((bf16[64,8,4,128]{3,0,2,1:T(8,128)(2,1)}), bf16[64,8,4,128]{3,0,2,1:T(8,128)(2,1)S(1)}, u32[]{:S(2)}, u32[]{:S(2)}) async-start(bf16[64,8,4,128]{3,0,2,1:T(8,128)(2,1)} %bitcast.5), calls=%async_computation | async-start | bytes 1048576 | tf_op jit(solution)/shard_map/all_to_all | solution.py:40
  176.7 31.7 %copy-start.2 = (bf16[64,1024]{1,0:T(8,128)(2,1)}, bf16[64,1024]{1,0:T(8,128)(2,1)S(1)}, u32[]{:S(2)}) copy-start(bf16[64,1024]{1,0:T(8,128)(2,1)S(1)} %convolution_convert_fusion) | copy-start | bytes 393220
where the time goes:
time: 252 us; the launch traced here: 251 us
  blocking collectives  187 us (74%)
  other arithmetic  28.7 us (11%)
  waiting for transfers between devices  11.9 us (5%)
  local copies, waits for them, and re-layouts  9.49 us (4%)
  matrix products  7.18 us (3%)
  starting transfers between devices  5.45 us (2%)
    psum x2, blocking collectives, shards(): gram = lax.psum(local_gram, ('dom', 'group')) / total_rows  84.7 us
    psum x1, blocking collectives, shards(): ritz = lax.psum(local_ritz, ('dom', 'group')) / total_rows  41.9 us
    all_to_all x2, blocking collectives, apply_graph(): lax.all_to_all(outgoing, 'dom', split_axis=1, concat_axis=1, tiled=True)  32.5 us
    all_gather x3, blocking collectives, apply_graph(): part_blocks = lax.all_gather(shaped, 'group', axis=1, tiled=True)  28.5 us
    another operation x6, other arithmetic, shards(): lower = jnp.linalg.cholesky(gram)  13 us
    all_to_all x1, waiting for transfers between devices, apply_graph(): lax.all_to_all(outgoing, 'dom', split_axis=1, concat_axis=1, tiled=True)  11.9 us
    another operation x4, other arithmetic, shards(): lax.linalg.triangular_solve(lower, rounded.astype(jnp.float32), left_side...  11.1 us
    gather x3, local copies, waits for them, and re-layouts, apply_graph(): picked = jnp.take(pool, pool_index, axis=1)  5.61 us
  transfers between devices with their start and end apart: 1, of which 1 were waited for; matrix products, arithmetic and copies ran while one was open for 0% of the time, Pallas kernels for 0%

commit v1 on v0

--- a/solution.py
+++ b/solution.py
@@ -58,7 +58,7 @@
     local_ritz = jnp.einsum(
         "kn,ln->kl", current.astype(jnp.float32), final, precision=lax.Precision.HIGHEST
     )
-    ritz = lax.psum(local_ritz, ("dom", "group")) / total_rows
+    ritz = jnp.sum(lax.all_gather(local_ritz, ("dom", "group")), axis=0) / total_rows
     return (current, ritz)
 
 

time: 252 us -> 285 us (1.13)
  the two profiles are of different devices: /device:TPU:14 before, /device:TPU:0 now
where the time goes in v1:
time: 285 us
  blocking collectives  218 us (76%)
  other arithmetic  28.8 us (10%)
  waiting for transfers between devices  15.1 us (5%)
  local copies, waits for them, and re-layouts  9.57 us (3%)
  matrix products  7.22 us (3%)
  starting transfers between devices  5.01 us (2%)
    psum x2, blocking collectives, shards(): gram = lax.psum(local_gram, ('dom', 'group')) / total_rows  74.5 us
    all_gather x1, blocking collectives, shards(): lax.all_gather(local_ritz, ('dom', 'group'))  70.9 us
    all_to_all x2, blocking collectives, apply_graph(): lax.all_to_all(outgoing, 'dom', split_axis=1, concat_axis=1, tiled=True)  38.2 us
    all_gather x3, blocking collectives, apply_graph(): part_blocks = lax.all_gather(shaped, 'group', axis=1, tiled=True)  34.5 us
    all_to_all x1, waiting for transfers between devices, apply_graph(): lax.all_to_all(outgoing, 'dom', split_axis=1, concat_axis=1, tiled=True)  15.1 us
    another operation x6, other arithmetic, shards(): lower = jnp.linalg.cholesky(gram)  13 us
    another operation x4, other arithmetic, shards(): lax.linalg.triangular_solve(lower, rounded.astype(jnp.float32), left_side...  11.1 us
  transfers between devices with their start and end apart: 1, of which 1 were waited for; matrix products, arithmetic and copies ran while one was open for 0% of the time, Pallas kernels for 0%

profile of v1, /device:TPU:0, one launch (start us, length us, event | category | flops | bytes accessed | tf_op | source)
XLA Modules:
  0.0 284.8 jit_solution(6644377734615638734)
XLA Ops:
  1.7 11.5 %all_gather.15 = bf16[64,32,128]{2,0,1:T(8,128)(2,1)S(1)} all-gather(bf16[64,8,128]{2,0,1:T(8,128)(2,1)S(1)} %copy_bitcast_fusion.2), channel_id=1, replica_groups=mesh['dom'=8,'group'=4] {'group'}, dimensions={1}, use_global_device_ids=true | all-gather | bytes 655360 | tf_op jit(solution)/shard_map/all_gather | solution.py:36
  13.8 0.9 broadcast_select_fusion.2
  14.7 5.0 %all-to-all-start = ((bf16[64,8,4,128]{3,0,2,1:T(8,128)(2,1)}), bf16[64,8,4,128]{3,0,2,1:T(8,128)(2,1)S(1)}, u32[]{:S(2)}, u32[]{:S(2)}) async-start(bf16[64,8,4,128]{3,0,2,1:T(8,128)(2,1)} %bitcast.5), calls=%async_computation | async-start | bytes 1048576 | tf_op jit(solution)/shard_map/all_to_all | solution.py:40
  20.0 15.1 %all-to-all-done = bf16[64,8,4,128]{3,0,2,1:T(8,128)(2,1)S(1)} async-done(((bf16[64,8,4,128]{3,0,2,1:T(8,128)(2,1)}), bf16[64,8,4,128]{3,0,2,1:T(8,128)(2,1)S(1)}, u32[]{:S(2)}, u32[]{:S(2)}) %all-to-all-start) | async-done | bytes 524320 | tf_op jit(solution)/shard_map/all_to_all | solution.py:40
  35.1 1.1 pad_maximum_fusion
  36.2 1.9 gather_fusion.1
  38.9 1.1 fusion.3
  40.1 37.0 %psum.14 = f32[64,64]{0,1:T(8,128)S(1)} all-reduce(f32[64,64]{0,1:T(8,128)S(1)} %convolution_bitcast_fusion.4), channel_id=1, replica_groups=mesh['dom'=8,'group'=4] {'dom','group'}, use_global_device_ids=true, to_apply=%region_0.3 | all-reduce | flops 4096 | bytes 32768 | tf_op jit(solution)/shard_map/psum | solution.py:52
  77.3 5.8 %cholesky.44 = f32[64,64]{1,0:T(8,128)S(1)} custom-call(f32[64,64]{1,0:T(8,128)S(1)} %fusion.35), custom_call_target="Cholesky" | custom-call | tf_op jit(solution)/shard_map/jit(cholesky)/cholesky | solution.py:53
  84.4 4.9 %custom-call.6 = f32[1,64,64]{1,2,0:T(8,128)S(1)} custom-call(f32[1,64,64]{2,1,0:T(8,128)S(1)} %fusion.30), custom_call_target="InvertDiagBlocksLowerTriangular" | custom-call | tf_op jit(solution)/shard_map/triangular_solve/custom-call.0 | solution.py:54
  89.8 11.5 %all_gather.16 = bf16[64,32,128]{2,0,1:T(8,128)(2,1)S(1)} all-gather(bf16[64,8,128]{2,0,1:T(8,128)(2,1)S(1)} %bitcast.127), channel_id=1, replica_groups=mesh['dom'=8,'group'=4] {'group'}, dimensions={1}, use_global_device_ids=true | all-gather | bytes 655360 | tf_op jit(solution)/shard_map/all_gather | solution.py:36
  102.1 19.3 %all_to_all.15 = bf16[64,8,4,128]{3,0,2,1:T(8,128)(2,1)S(1)} all-to-all(bf16[64,8,4,128]{3,0,2,1:T(8,128)(2,1)S(1)} %bitcast.120), channel_id=1, replica_groups=mesh['dom'=8,'group'=4] {'dom'}, dimensions={1} | all-to-all | bytes 1048576 | tf_op jit(solution)/shard_map/all_to_all | solution.py:40
  121.4 1.1 pad_maximum_fusion.1
  122.5 1.9 gather_fusion.3
  125.2 1.1 fusion.2
  126.5 37.6 %psum.15 = f32[64,64]{0,1:T(8,128)S(1)} all-reduce(f32[64,64]{0,1:T(8,128)S(1)} %convolution_bitcast_fusion.3), channel_id=1, replica_groups=mesh['dom'=8,'group'=4] {'dom','group'}, use_global_device_ids=true, to_apply=%region_3.0 | all-reduce | flops 4096 | bytes 32768 | tf_op jit(solution)/shard_map/psum | solution.py:52
  164.2 5.8 %cholesky.55 = f32[64,64]{1,0:T(8,128)S(1)} custom-call(f32[64,64]{1,0:T(8,128)S(1)} %fusion.33), custom_call_target="Cholesky" | custom-call | tf_op jit(solution)/shard_map/jit(cholesky)/cholesky | solution.py:53
  171.4 4.9 %custom-call.7 = f32[1,64,64]{1,2,0:T(8,128)S(1)} custom-call(f32[1,64,64]{2,1,0:T(8,128)S(1)} %fusion.31), custom_call_target="InvertDiagBlocksLowerTriangular" | custom-call | tf_op jit(solution)/shard_map/triangular_solve/custom-call.0 | solution.py:54
  176.8 11.5 %all_gather.17 = bf16[64,32,128]{2,0,1:T(8,128)(2,1)S(1)} all-gather(bf16[64,8,128]{2,0,1:T(8,128)(2,1)S(1)} %copy_bitcast_fusion), channel_id=1, replica_groups=mesh['dom'=8,'group'=4] {'group'}, dimensions={1}, use_global_device_ids=true | all-gather | bytes 655360 | tf_op jit(solution)/shard_map/all_gather | solution.py:36
  189.0 18.8 %all_to_all.16 = bf16[64,8,4,128]{3,0,2,1:T(8,128)(2,1)S(1)} all-to-all(bf16[64,8,4,128]{3,0,2,1:T(8,128)(2,1)S(1)} %bitcast.119), channel_id=1, replica_groups=mesh['dom'=8,'group'=4] {'dom'}, dimensions={1} | all-to-all | bytes 1048576 | tf_op jit(solution)/shard_map/all_to_all | solution.py:40
  207.8 1.1 pad_maximum_fusion.2
  208.9 1.9 gather_fusion.5
  211.6 1.1 convolution_multiply_fusion
  213.0 70.9 %all-gather = f32[2048,64]{1,0:T(8,128)S(1)} all-gather(f32[64,64]{1,0:T(8,128)S(1)} %fusion.18), channel_id=2, replica_groups=mesh['dom'=8,'group'=4] {'dom','group'}, dimensions={0}, use_global_device_ids=true | all-gather | bytes 540672 | tf_op jit(solution)/shard_map/all_gather | solution.py:61
  (55 shorter events, 11.2 us)
Async XLA Ops:
  0.6 1.0 copy-start
  0.6 19.1 %copy-start.5 = (s32[1,32]{1,0:T(1,128)S(1)}, s32[1,32]{1,0:T(1,128)}, u32[]{:S(2)}) copy-start(s32[1,32]{1,0:T(1,128)} %param.17) | copy-start | bytes 388
  0.7 19.1 %copy-start.4 = (s32[1,32]{1,0:T(1,128)S(1)}, s32[1,32]{1,0:T(1,128)}, u32[]{:S(2)}) copy-start(s32[1,32]{1,0:T(1,128)} %param.16) | copy-start | bytes 388
  0.7 19.1 %copy-start.3 = (s32[1,9]{1,0:T(1,128)S(1)}, s32[1,9]{1,0:T(1,128)}, u32[]{:S(2)}) copy-start(s32[1,9]{1,0:T(1,128)} %param.15) | copy-start | bytes 112
  14.7 23.3 %copy-start.1 = (s32[1,32,128,128]{3,2,1,0:T(8,128)S(1)}, s32[1,32,128,128]{3,2,1,0:T(8,128)}, u32[]{:S(2)}) copy-start(s32[1,32,128,128]{3,2,1,0:T(8,128)} %param.14) | copy-start | bytes 6291460
  14.7 20.3 %all-to-all-start = ((bf16[64,8,4,128]{3,0,2,1:T(8,128)(2,1)}), bf16[64,8,4,128]{3,0,2,1:T(8,128)(2,1)S(1)}, u32[]{:S(2)}, u32[]{:S(2)}) async-start(bf16[64,8,4,128]{3,0,2,1:T(8,128)(2,1)} %bitcast.5), calls=%async_computation | async-start | bytes 1048576 | tf_op jit(solution)/shard_map/all_to_all | solution.py:40
  176.7 36.0 %copy-start.2 = (bf16[64,1024]{1,0:T(8,128)(2,1)}, bf16[64,1024]{1,0:T(8,128)(2,1)S(1)}, u32[]{:S(2)}) copy-start(bf16[64,1024]{1,0:T(8,128)(2,1)S(1)} %convolution_convert_fusion) | copy-start | bytes 393220
